TPU v7x, 128 devices: a whole 4x4x4 slice. The times are simulated.
128 devices in a mesh: rx: 8 (over x, core), ry: 16 (over y, z).
Axes of the slice: x: 4, y: 4, z: 4, core: 2. Of those that a mesh axis runs over, the one named last changes fastest.
Arguments:
- column_features: bfloat16 [16384, 1536], P(('rx', 'ry')), may hold values from -6 to 6
- column_route: int32 [16384], P(('rx', 'ry')), may hold values from 0 to 32767, as said below
- cotangent: bfloat16 [128, 256, 1536], P('rx', 'ry'), may hold values from -6 to 6
- first_weight: bfloat16 [27, 96, 96], replicated, may hold values from -0.125 to 0.125
- second_weight: bfloat16 [27, 96, 96], replicated, may hold values from -0.125 to 0.125
Outputs:
- block_output: bfloat16 [128, 256, 1536], P('rx', 'ry')
- feature_grads: bfloat16 [16384, 1536], P(('rx', 'ry'))
- first_grad: float32 [27, 96, 96], replicated
- second_grad: float32 [27, 96, 96], replicated
Inputs may be any that keep to these rules, and one draw needn't show every extreme that they name: `column_route`: entries are distinct; entry o * 256 + q names slot q of owner o, owner o = i * 16 + j being the device at rx index i and ry index j. The columns of one owner are spread over the devices' shards as evenly as possible: each shard holds the floor or the ceiling of that owner's count / 128. An owner holds at most 256 columns, and in every draw one owner holds exactly 256, so that it receives 2 from every shard.
All inputs are finite; a program needn't handle non-finite values.
Results may differ from a plain program's by a relative error of at most 0.0029.
Values may be sent and summed in bfloat16 or wider, within the bound.
A program may use at most 256 MiB of HBM per device.

v0:
```python
import jax
import jax.numpy as jnp
from jax import lax
from jax.sharding import PartitionSpec as P


def extended(block, sides, width):
    for axis, dim in sides:
        count = lax.axis_size(axis)
        forward = [(i, i + 1) for i in range(count - 1)]
        backward = [(target, source) for source, target in forward]
        low = lax.ppermute(
            lax.slice_in_dim(block, block.shape[dim] - width, None, axis=dim), axis, forward
        )
        high = lax.ppermute(lax.slice_in_dim(block, 0, width, axis=dim), axis, backward)
        block = jnp.concatenate([low, block, high], axis=dim)
    return block


def pad_depth(widened, channels):
    shaped = widened.reshape(
        widened.shape[0], widened.shape[1], widened.shape[2] // channels, channels
    )
    return jnp.pad(shaped, ((0, 0), (0, 0), (1, 1), (0, 0)))


def face_field(rows, channels):
    widened = extended(rows, (("rx", 0), ("ry", 1)), 1)
    return pad_depth(widened, channels)


def conv_sum(padded, weights):
    size_x = padded.shape[0] - 2
    size_y = padded.shape[1] - 2
    size_z = padded.shape[2] - 2
    result = jnp.zeros((size_x, size_y, size_z, weights.shape[1]), jnp.float32)
    for a in range(3):
        for b in range(3):
            for c in range(3):
                piece = padded[a : a + size_x, b : b + size_y, c : c + size_z, :]
                result = result + jnp.einsum(
                    "xyzi,oi->xyzo",
                    piece,
                    weights[9 * a + 3 * b + c],
                    preferred_element_type=jnp.float32,
                )
    return result


def correlate(grads, padded):
    size_x, size_y, size_z, _ = grads.shape
    terms = []
    for a in range(3):
        for b in range(3):
            for c in range(3):
                piece = padded[a : a + size_x, b : b + size_y, c : c + size_z, :]
                terms.append(
                    jnp.einsum("xyzo,xyzi->oi", grads, piece, preferred_element_type=jnp.float32)
                )
    return jnp.stack(terms, axis=0)


def flipped(weights):
    return jnp.transpose(weights[::-1], (0, 2, 1))


def on_device(column_features, column_route, cotangent, first_weight, second_weight):
    count_x = lax.axis_size("rx")
    count_y = lax.axis_size("ry")
    count_all = count_x * count_y
    shard_rows = column_features.shape[0]
    row_width = column_features.shape[1]
    region_x = cotangent.shape[0]
    region_y = cotangent.shape[1]
    channels = first_weight.shape[1]
    depth = row_width // channels
    region_slots = region_x * region_y
    capacity = 2 * shard_rows // count_all
    owners = column_route // region_slots
    slot_ids = column_route % region_slots
    shard_index = jnp.arange(shard_rows, dtype=jnp.int32)
    earlier = shard_index[:, None] > shard_index[None, :]
    same_owner = owners[:, None] == owners[None, :]
    ranks = jnp.sum(jnp.logical_and(earlier, same_owner).astype(jnp.int32), axis=1)
    send_pos = owners * capacity + ranks
    buffer_index = jnp.arange(count_all * capacity, dtype=jnp.int32)
    send_hot = send_pos[:, None] == buffer_index[None, :]
    send_table = send_hot.astype(jnp.bfloat16)
    outgoing = jnp.einsum(
        "sr,sw->rw", send_table, column_features, preferred_element_type=jnp.float32
    ).astype(jnp.bfloat16)
    filled = jnp.sum(send_hot.astype(jnp.int32), axis=0)
    slot_total = jnp.sum(jnp.where(send_hot, slot_ids[:, None], 0), axis=0)
    out_slots = jnp.where(filled > 0, slot_total, region_slots)
    incoming, in_slots = (
        lax.all_to_all(
            outgoing.reshape(count_all, capacity, row_width),
            ("rx", "ry"),
            split_axis=0,
            concat_axis=0,
            tiled=True,
        ),
        lax.all_to_all(
            out_slots.reshape(count_all, capacity),
            ("rx", "ry"),
            split_axis=0,
            concat_axis=0,
            tiled=True,
        ),
    )
    incoming = incoming.reshape(count_all * capacity, row_width)
    in_slots = in_slots.reshape(count_all * capacity)
    slot_hot = in_slots[:, None] == jnp.arange(region_slots, dtype=jnp.int32)[None, :]
    slot_table = slot_hot.astype(jnp.bfloat16)
    region_rows = jnp.einsum(
        "rs,rw->sw", slot_table, incoming, preferred_element_type=jnp.float32
    ).astype(jnp.bfloat16)
    active = jnp.sum(slot_hot.astype(jnp.float32), axis=0)
    field = jnp.transpose(region_rows.reshape(region_x, region_y, channels, depth), (0, 1, 3, 2))
    mask = active.reshape(region_x, region_y, 1, 1)
    cot_field = jnp.transpose(
        cotangent.reshape(region_x, region_y, channels, depth), (0, 1, 3, 2)
    ).astype(jnp.float32)
    outer_grad = (mask * cot_field).astype(jnp.bfloat16)
    field_flat = field.reshape(region_x, region_y, row_width)
    outer_flat = outer_grad.reshape(region_x, region_y, row_width)
    padded_x = pad_depth(extended(field_flat, (("rx", 0), ("ry", 1)), 1), channels)
    padded_g = pad_depth(extended(outer_flat, (("rx", 0), ("ry", 1)), 1), channels)
    hidden = mask * conv_sum(padded_x, first_weight)
    act = jax.nn.silu(hidden).astype(jnp.bfloat16)
    padded_a = face_field(act.reshape(region_x, region_y, row_width), channels)
    second = conv_sum(padded_a, second_weight)
    summed = (field.astype(jnp.float32) + mask * second).astype(jnp.bfloat16)
    block_output = jnp.transpose(summed, (0, 1, 3, 2)).reshape(region_x, region_y, row_width)
    act_grad = conv_sum(padded_g, flipped(second_weight))
    sigma = jax.nn.sigmoid(hidden)
    hidden_grad = (mask * act_grad * sigma * (1.0 + hidden * (1.0 - sigma))).astype(jnp.bfloat16)
    padded_h = face_field(hidden_grad.reshape(region_x, region_y, row_width), channels)
    grid_grad = (mask * cot_field + conv_sum(padded_h, flipped(first_weight))).astype(jnp.bfloat16)
    grad_rows = jnp.transpose(grid_grad, (0, 1, 3, 2)).reshape(region_slots, row_width)
    backward = jnp.dot(slot_table, grad_rows, preferred_element_type=jnp.float32).astype(
        jnp.bfloat16
    )
    returned = lax.all_to_all(
        backward.reshape(count_all, capacity, row_width),
        ("rx", "ry"),
        split_axis=0,
        concat_axis=0,
        tiled=True,
    )
    returned_rows = returned.reshape(count_all * capacity, row_width)
    feature_grads = jnp.dot(send_table, returned_rows, preferred_element_type=jnp.float32).astype(
        jnp.bfloat16
    )
    second_local = correlate(outer_grad, padded_a)
    first_local = correlate(hidden_grad, padded_x)
    first_total, second_total = lax.psum((first_local, second_local), ("rx", "ry"))
    factor = 1.0 / jnp.sqrt(jnp.float32(count_all * shard_rows * depth))
    return (block_output, feature_grads, first_total * factor, second_total * factor)


def solution(mesh):
    in_specs = (P(("rx", "ry"), None), P(("rx", "ry")), P("rx", "ry", None), P(), P())
    out_specs = (P("rx", "ry", None), P(("rx", "ry"), None), P(), P())
    return jax.shard_map(
        on_device, mesh=mesh, in_specs=in_specs, out_specs=out_specs, check_vma=False
    )
```

profile of v0, /device:TPU:1, one launch (start us, length us, event | category | flops | bytes accessed | tf_op | source)
XLA Modules:
  0.0 670.0 jit_solution(15882649967225699093)
XLA Ops:
  9.0 11.5 %all-to-all-start = ((s32[128,1,2]{2,1,0:T(1,128)}), s32[128,1,2]{2,1,0:T(1,128)S(1)}, u32[]{:S(2)}, u32[]{:S(2)}) async-start(s32[128,1,2]{2,1,0:T(1,128)} %bitcast), calls=%async_computation | async-start | bytes 131072 | tf_op jit(solution)/shard_map/all_to_all | solution.py:103
  21.0 2.2 copy.39
  24.4 6.9 %reshape.118 = f32[16,16,96,16]{3,2,1,0:T(8,128)} reshape(bf16[16,16,1536]{2,1,0:T(8,128)(2,1)S(1)} %copy-done.16) | data formatting | bytes 2359296 | tf_op jit(solution)/shard_map/convert_element_type | solution.py:123
  31.2 8.4 %copy.37 = f32[16,16,96,16]{2,3,1,0:T(8,128)S(1)} copy(f32[16,16,96,16]{3,2,1,0:T(8,128)} %reshape.118) | data formatting | bytes 3145728 | tf_op jit(solution)/shard_map/convert_element_type | solution.py:123
  39.7 10.2 %all-to-all-start.1 = ((bf16[128,2,1536]{2,1,0:T(2,128)(2,1)}), bf16[128,2,1536]{2,1,0:T(2,128)(2,1)}, u32[]{:S(2)}, u32[]{:S(2)}) async-start(bf16[128,2,1536]{2,1,0:T(2,128)(2,1)} %reshape.103), calls=%async_computation.1 | async-start | bytes 1572864 | tf_op jit(solution)/shard_map/all_to_all | solution.py:96
  52.0 3.5 collective-permute-start.8
  55.6 2.0 reverse_bitcast_fusion
  60.3 1.9 collective-permute-start.9
  62.3 3.8 collective-permute-done.9
  66.3 3.1 collective-permute-start.10
  71.8 3.1 collective-permute-done.11
  76.7 2.6 fusion.61
  86.5 1.8 fusion.66
  93.7 1.8 fusion.70
  95.5 1.8 fusion.71
  97.3 1.8 fusion.72
  115.0 1.8 fusion.75
  120.4 2.3 reshape.104
  123.2 6.8 %reshape.105 = bf16[16,16,96,16]{3,2,1,0:T(8,128)(2,1)} reshape(bf16[256,1536]{1,0:T(8,128)(2,1)S(1)} %convolution_convert_fusion.2) | data formatting | bytes 1572864 | tf_op jit(solution)/shard_map/reshape | solution.py:119
  132.0 3.9 collective-permute-start
  136.0 2.5 fusion.76
  138.5 6.0 copy.34
  144.9 1.9 collective-permute-start.1
  150.5 3.4 collective-permute-start.2
  155.1 2.5 fusion.60
  157.7 6.1 copy.32
  165.5 2.7 reshape.107
  168.3 2.6 fusion.114
  172.7 1.8 fusion.116
  178.1 1.9 fusion.119
  187.1 1.8 fusion.124
  192.5 1.8 fusion.127
  203.2 1.9 fusion.220
  215.7 20.1 %multiply_convert_fusion.1 = (bf16[16,16,16,96]{3,2,1,0:T(8,128)(2,1)}, f32[16,16,16,96]{3,2,1,0:T(8,128)}) fusion(bf16[27,96,96]{2,1,0:T(8,128)(2,1)} %param.8, bf16[18,18,16,96]{3,2,1,0:T(8,128)(2,1)S(1)} %reshape.107, f32[16,16,16,96]{3,2,1,0:T(8,128)} %fusion.208, f32[16,16,16,96]{3,2,1,0:T(8,128)} %fusion.129, f32[16,16,16,96]{3,2,1,0:T(8,128)} %fusion.128, ...), kind=kOutput, calls=%fused_computation.102 | convolution fusion | flops 88080384 | bytes 57906176 | tf_op jit(solution)/shard_map/xyzi,oi->xyzo/dot_general | solution.py:41
  235.8 20.1 %multiply_convert_fusion = bf16[16,16,16,96]{3,2,1,0:T(8,128)(2,1)} fusion(f32[16,16,16,96]{3,2,1,0:T(8,128)} %get-tuple-element.27, f32[16,16,16,96]{3,2,1,0:T(8,128)} %fusion.162, f32[16,16,16,96]{3,2,1,0:T(8,128)} %fusion.76, f32[16,16,16,96]{3,2,1,0:T(8,128)} %fusion.75, f32[16,16,16,96]{3,2,1,0:T(8,128)} %fusion.163, f32[16,16,16,96]{3,2,1,0:T(8,128)} %fusion.74, ...), kind=kOutput, calls=%fused_computation.101 | convolution fusion | flops 89653248 | bytes 58430464 | tf_op jit(solution)/shard_map/xyzi,oi->xyzo/dot_general | solution.py:41
  256.8 2.4 fusion.58
  259.4 2.5 collective-permute-start.4
  262.0 3.2 collective-permute-start.12
  265.3 2.3 fusion.57
  298.4 1.9 collective-permute-start.5
  300.4 1.9 collective-permute-start.13
  304.0 4.0 collective-permute-start.6
  309.6 4.9 collective-permute-start.14
  317.6 2.6 fusion.132
  338.0 1.8 fusion.143
  345.2 1.8 fusion.147
  350.5 1.8 fusion.180
  352.3 1.8 fusion.184
  367.8 2.9 reshape.114
  370.7 2.6 fusion.79
  384.0 1.8 fusion.86
  387.6 1.9 fusion.88
  393.0 1.8 fusion.91
  396.6 1.8 fusion.93
  410.9 1.9 fusion.159
  447.1 19.9 %fusion.1 = bf16[16,16,96,16]{2,3,1,0:T(8,128)(2,1)} fusion(f32[16,16,16,96]{3,2,1,0:T(8,128)} %fusion.153, f32[16,16,16,96]{3,2,1,0:T(8,128)} %fusion.94, f32[16,16,16,96]{3,2,1,0:T(8,128)} %fusion.93, f32[16,16,16,96]{3,2,1,0:T(8,128)} %fusion.154, f32[16,16,16,96]{3,2,1,0:T(8,128)} %fusion.92, f32[16,16,16,96]{3,2,1,0:T(8,128)} %fusion.91, ...), kind=kOutput, calls=%fused_computation.78 | convolution fusion | flops 86900736 | bytes 58430464 | tf_op jit(solution)/shard_map/xyzi,oi->xyzo/dot_general | solution.py:41
  466.9 6.0 copy.40
  472.9 11.3 %reshape.115 = bf16[256,1536]{1,0:T(8,128)(2,1)S(1)} reshape(bf16[16,16,96,16]{3,2,1,0:T(8,128)(2,1)} %copy.40) | data formatting | bytes 1572864 | tf_op jit(solution)/shard_map/reshape | solution.py:140
  485.9 13.1 %all-to-all-start.2 = ((bf16[128,2,1536]{2,1,0:T(2,128)(2,1)}), bf16[128,2,1536]{2,1,0:T(2,128)(2,1)S(1)}, u32[]{:S(2)}, u32[]{:S(2)}) async-start(bf16[128,2,1536]{2,1,0:T(2,128)(2,1)} %reshape.116), calls=%async_computation.2 | async-start | bytes 1572864 | tf_op jit(solution)/shard_map/all_to_all | solution.py:144
  499.8 19.6 %fusion.4 = bf16[16,16,96,16]{2,3,1,0:T(8,128)(2,1)} fusion(f32[16,16,16,96]{3,2,1,0:T(8,128)} %fusion.172, f32[16,16,16,96]{3,2,1,0:T(8,128)} %fusion.147, f32[16,16,16,96]{3,2,1,0:T(8,128)} %fusion.146, f32[16,16,16,96]{3,2,1,0:T(8,128)} %fusion.176, f32[16,16,16,96]{3,2,1,0:T(8,128)} %fusion.145, f32[16,16,16,96]{3,2,1,0:T(8,128)} %fusion.144, ...), kind=kOutput, calls=%fused_computation.91 | convolution fusion | flops 87293952 | bytes 57119744 | tf_op jit(solution)/shard_map/xyzi,oi->xyzo/dot_general | solution.py:41
  519.4 6.0 copy.36
  525.4 11.8 %reshape.110 = bf16[16,16,1536]{2,1,0:T(8,128)(2,1)} reshape(bf16[16,16,96,16]{3,2,1,0:T(8,128)(2,1)} %copy.36) | data formatting | bytes 1572864 | tf_op jit(solution)/shard_map/reshape | solution.py:134
  538.6 120.6 %all-reduce.7.cloned.1.call-done = (f32[27,96,96]{2,1,0:T(8,128)}, f32[27,96,96]{2,1,0:T(8,128)}) async-done(((f32[27,96,96]{2,1,0:T(8,128)}, f32[27,96,96]{2,1,0:T(8,128)}), (f32[27,96,96]{2,1,0:T(8,128)}, f32[27,96,96]{2,1,0:T(8,128)})) %all-reduce.7.cloned.1.call-update) | async-done | bytes 1990672 | tf_op jit(solution)/shard_map/psum | solution.py:157
  659.2 3.5 broadcast_multiply_fusion
  (261 shorter events, 236.6 us)
Async XLA Ops:
  7.2 13.3 %copy-start = (bf16[128,1536]{1,0:T(8,128)(2,1)S(1)}, bf16[128,1536]{1,0:T(8,128)(2,1)}, u32[]{:S(2)}) copy-start(bf16[128,1536]{1,0:T(8,128)(2,1)} %param.5) | copy-start | bytes 1179652
  8.1 16.3 %copy-start.21 = (s32[128]{0:T(128)}, s32[128]{0:T(128)S(1)}, u32[]{:S(2)}) copy-start(s32[128]{0:T(128)S(1)} %multiply_add_fusion) | copy-start | bytes 1540
  9.0 30.7 %all-to-all-start = ((s32[128,1,2]{2,1,0:T(1,128)}), s32[128,1,2]{2,1,0:T(1,128)S(1)}, u32[]{:S(2)}, u32[]{:S(2)}) async-start(s32[128,1,2]{2,1,0:T(1,128)} %bitcast), calls=%async_computation | async-start | bytes 131072 | tf_op jit(solution)/shard_map/all_to_all | solution.py:103
  20.5 3.8 copy-start.16
  39.6 12.2 %copy-start.2 = (f32[16,16,96,16]{2,3,1,0:T(8,128)}, f32[16,16,96,16]{2,3,1,0:T(8,128)S(1)}, u32[]{:S(2)}) copy-start(f32[16,16,96,16]{2,3,1,0:T(8,128)S(1)} %copy.37) | copy-start | bytes 4718596
  39.7 80.8 %all-to-all-start.1 = ((bf16[128,2,1536]{2,1,0:T(2,128)(2,1)}), bf16[128,2,1536]{2,1,0:T(2,128)(2,1)}, u32[]{:S(2)}, u32[]{:S(2)}) async-start(bf16[128,2,1536]{2,1,0:T(2,128)(2,1)} %reshape.103), calls=%async_computation.1 | async-start | bytes 1572864 | tf_op jit(solution)/shard_map/all_to_all | solution.py:96
  51.3 71.4 %copy-start.19 = (s32[256]{0:T(256)}, s32[256]{0:T(256)S(1)}, u32[]{:S(2)}) copy-start(s32[256]{0:T(256)S(1)} %eq.49) | copy-start | bytes 3076
  51.5 6.0 copy-start.17
  51.9 8.3 %copy-start.6 = (bf16[16,16,16,96]{3,2,1,0:T(8,128)(2,1)}, bf16[16,16,16,96]{3,2,1,0:T(8,128)(2,1)S(1)}, u32[]{:S(2)}) copy-start(bf16[16,16,16,96]{3,2,1,0:T(8,128)(2,1)S(1)} %fusion.59) | copy-start | bytes 2359300
  52.0 10.2 %collective-permute-start.8 = (bf16[1,16,1536]{2,1,0:T(8,128)(2,1)S(1)}, bf16[1,16,1536]{2,1,0:T(8,128)(2,1)S(1)}, u32[]{:S(2)}, u32[]{:S(2)}) collective-permute-start(bf16[1,16,1536]{2,1,0:T(8,128)(2,1)S(1)} %slice.931), channel_id=1, source_target_pairs={{0,16},{16,32},{32,48},{48,64},{64,80},{80,96},{96,112},{1,17},{17... | collective-permute-start | bytes 147464 | tf_op jit(solution)/shard_map/ppermute | solution.py:12
  60.3 5.8 collective-permute-start.9
  66.3 5.5 collective-permute-start.10
  69.4 5.5 collective-permute-start.11
  76.7 2.6 copy-start.13
  132.0 16.0 %collective-permute-start = (bf16[1,16,1536]{2,1,0:T(8,128)(2,1)}, bf16[1,16,1536]{2,1,0:T(8,128)(2,1)}, u32[]{:S(2)}, u32[]{:S(2)}) collective-permute-start(bf16[1,16,1536]{2,1,0:T(8,128)(2,1)} %slice.811), channel_id=1, source_target_pairs={{0,16},{16,32},{32,48},{48,64},{64,80},{80,96},{96,112},{1,17},{17... | collective-permute-start | bytes 147464 | tf_op jit(solution)/shard_map/ppermute | solution.py:12
  144.9 5.4 collective-permute-start.1
  150.5 13.3 %collective-permute-start.2 = (bf16[18,1,1536]{2,1,0:T(2,128)(2,1)S(1)}, bf16[18,1,1536]{2,1,0:T(2,128)(2,1)S(1)}, u32[]{:S(2)}, u32[]{:S(2)}) collective-permute-start(bf16[18,1,1536]{2,1,0:T(2,128)(2,1)S(1)} %get-tuple-element.22), channel_id=1, source_target_pairs={{0,1},{1,2},{2,3},{3,4},{4,5},{5,6},{6,7},{7,8},{8,9},{9,10},{10,1... | collective-permute-start | bytes 165896 | tf_op jit(solution)/shard_map/ppermute | solution.py:12
  153.8 10.0 %collective-permute-start.3 = (bf16[18,1,1536]{2,1,0:T(2,128)(2,1)S(1)}, bf16[18,1,1536]{2,1,0:T(2,128)(2,1)S(1)}, u32[]{:S(2)}, u32[]{:S(2)}) collective-permute-start(bf16[18,1,1536]{2,1,0:T(2,128)(2,1)S(1)} %get-tuple-element.23), channel_id=1, source_target_pairs={{1,0},{2,1},{3,2},{4,3},{5,4},{6,5},{7,6},{8,7},{9,8},{10,9},{11,1... | collective-permute-start | bytes 165896 | tf_op jit(solution)/shard_map/ppermute | solution.py:15
  168.3 2.6 copy-start.10
  213.9 1.8 copy-start.18
  256.8 2.5 copy-start.3
  259.4 43.0 %collective-permute-start.4 = (bf16[1,16,1536]{2,1,0:T(8,128)(2,1)S(1)}, bf16[1,16,1536]{2,1,0:T(8,128)(2,1)S(1)}, u32[]{:S(2)}, u32[]{:S(2)}) collective-permute-start(bf16[1,16,1536]{2,1,0:T(8,128)(2,1)S(1)} %slice.871), channel_id=1, source_target_pairs={{0,16},{16,32},{32,48},{48,64},{64,80},{80,96},{96,112},{1,17},{17... | collective-permute-start | bytes 147464 | tf_op jit(solution)/shard_map/ppermute | solution.py:12
  262.0 5.5 copy-start.4
  262.0 47.2 %collective-permute-start.12 = (bf16[1,16,1536]{2,1,0:T(8,128)(2,1)S(1)}, bf16[1,16,1536]{2,1,0:T(8,128)(2,1)S(1)}, u32[]{:S(2)}, u32[]{:S(2)}) collective-permute-start(bf16[1,16,1536]{2,1,0:T(8,128)(2,1)S(1)} %slice.991), channel_id=1, source_target_pairs={{0,16},{16,32},{32,48},{48,64},{64,80},{80,96},{96,112},{1,17},{17... | collective-permute-start | bytes 147464 | tf_op jit(solution)/shard_map/ppermute | solution.py:12
  295.8 1.2 copy-start.5
  298.4 5.4 collective-permute-start.5
  300.4 8.9 %collective-permute-start.13 = (bf16[1,16,1536]{2,1,0:T(8,128)(2,1)S(1)}, bf16[1,16,1536]{2,1,0:T(8,128)(2,1)S(1)}, u32[]{:S(2)}, u32[]{:S(2)}) collective-permute-start(bf16[1,16,1536]{2,1,0:T(8,128)(2,1)S(1)} %slice.993), channel_id=1, source_target_pairs={{16,0},{32,16},{48,32},{64,48},{80,64},{96,80},{112,96},{17,1},{33... | collective-permute-start | bytes 147464 | tf_op jit(solution)/shard_map/ppermute | solution.py:15
  304.0 11.8 %collective-permute-start.6 = (bf16[18,1,1536]{2,1,0:T(2,128)(2,1)S(1)}, bf16[18,1,1536]{2,1,0:T(2,128)(2,1)S(1)}, u32[]{:S(2)}, u32[]{:S(2)}) collective-permute-start(bf16[18,1,1536]{2,1,0:T(2,128)(2,1)S(1)} %get-tuple-element.20), channel_id=1, source_target_pairs={{0,1},{1,2},{2,3},{3,4},{4,5},{5,6},{6,7},{7,8},{8,9},{9,10},{10,1... | collective-permute-start | bytes 165896 | tf_op jit(solution)/shard_map/ppermute | solution.py:12
  308.0 7.8 %collective-permute-start.7 = (bf16[18,1,1536]{2,1,0:T(2,128)(2,1)S(1)}, bf16[18,1,1536]{2,1,0:T(2,128)(2,1)S(1)}, u32[]{:S(2)}, u32[]{:S(2)}) collective-permute-start(bf16[18,1,1536]{2,1,0:T(2,128)(2,1)S(1)} %get-tuple-element.21), channel_id=1, source_target_pairs={{1,0},{2,1},{3,2},{4,3},{5,4},{6,5},{7,6},{8,7},{9,8},{10,9},{11,1... | collective-permute-start | bytes 165896 | tf_op jit(solution)/shard_map/ppermute | solution.py:15
  309.4 6.4 copy-start.14
  309.6 56.5 %collective-permute-start.14 = (bf16[18,1,1536]{2,1,0:T(2,128)(2,1)S(1)}, bf16[18,1,1536]{2,1,0:T(2,128)(2,1)S(1)}, u32[]{:S(2)}, u32[]{:S(2)}) collective-permute-start(bf16[18,1,1536]{2,1,0:T(2,128)(2,1)S(1)} %get-tuple-element.16), channel_id=1, source_target_pairs={{0,1},{1,2},{2,3},{3,4},{4,5},{5,6},{6,7},{7,8},{8,9},{9,10},{10,1... | collective-permute-start | bytes 165896 | tf_op jit(solution)/shard_map/ppermute | solution.py:12
  314.4 51.6 %collective-permute-start.15 = (bf16[18,1,1536]{2,1,0:T(2,128)(2,1)S(1)}, bf16[18,1,1536]{2,1,0:T(2,128)(2,1)S(1)}, u32[]{:S(2)}, u32[]{:S(2)}) collective-permute-start(bf16[18,1,1536]{2,1,0:T(2,128)(2,1)S(1)} %get-tuple-element.17), channel_id=1, source_target_pairs={{1,0},{2,1},{3,2},{4,3},{5,4},{6,5},{7,6},{8,7},{9,8},{10,9},{11,1... | collective-permute-start | bytes 165896 | tf_op jit(solution)/shard_map/ppermute | solution.py:15
  317.6 2.6 copy-start.11
  361.3 1.8 copy-start.7
  364.2 1.8 copy-start.15
  370.7 2.6 copy-start.12
  416.3 1.8 copy-start.8
  472.9 11.3 %copy-start.20 = (s32[256]{0:T(256)S(1)}, s32[256]{0:T(256)}, u32[]{:S(2)}) copy-start(s32[256]{0:T(256)} %copy-done.19) | copy-start | bytes 3076
  485.9 13.9 %copy-start.9 = (bf16[16,16,96,16]{2,3,1,0:T(8,128)(2,1)S(1)}, bf16[16,16,96,16]{2,3,1,0:T(8,128)(2,1)}, u32[]{:S(2)}) copy-start(bf16[16,16,96,16]{2,3,1,0:T(8,128)(2,1)} %copy.32) | copy-start | bytes 2359300
  485.9 51.3 %all-to-all-start.2 = ((bf16[128,2,1536]{2,1,0:T(2,128)(2,1)}), bf16[128,2,1536]{2,1,0:T(2,128)(2,1)S(1)}, u32[]{:S(2)}, u32[]{:S(2)}) async-start(bf16[128,2,1536]{2,1,0:T(2,128)(2,1)} %reshape.116), calls=%async_computation.2 | async-start | bytes 1572864 | tf_op jit(solution)/shard_map/all_to_all | solution.py:144
  499.0 160.2 %all-reduce.7.cloned.1.call-start = ((), (), s32[]{:S(2)}) async-start(), calls=%async_computation.3 | async-start | bytes 5308416 | tf_op jit(solution)/shard_map/psum | solution.py:157
  525.4 12.1 %copy-start.22 = (s32[128]{0:T(128)S(1)}, s32[128]{0:T(128)}, u32[]{:S(2)}) copy-start(s32[128]{0:T(128)} %copy-done.21) | copy-start | bytes 1540
  659.2 3.5 copy-start.1
Sparse Core Ops, SparseCore 0:
  505.5 153.6 all-reduce.6
where the time goes:
time: 677 us; the launch traced here: 670 us
  matrix products  336 us (50%)
  waiting for transfers between devices  131 us (19%)
  local copies, waits for them, and re-layouts  101 us (15%)
  starting transfers between devices  76.5 us (11%)
  between operations  15.2 us (2%)
  other arithmetic  10.5 us (2%)
    dot_general x108, matrix products, conv_sum(): jnp.einsum('xyzi,oi->xyzo', piece, weights[9 * a + 3 * b + c], preferred_...  270 us
    psum x1, waiting for transfers between devices, on_device(): lax.psum((first_local, second_local), ('rx', 'ry'))  121 us
    dot_general x54, matrix products, correlate(): jnp.einsum('xyzo,xyzi->oi', grads, piece, preferred_element_type=jnp.floa...  63.1 us
    ppermute x8, starting transfers between devices, extended(): lax.ppermute(lax.slice_in_dim(block, block.shape[dim] - width, None, axis...  28.5 us
    convert_element_type x2, local copies, waits for them, and re-layouts, on_device(): cot_field = jnp.transpose(cotangent.reshape(region_x, region_y, channels,...  15.3 us
  transfers between devices with their start and end apart: 20, of which 5 were waited for; matrix products, arithmetic and copies ran while one was open for 32% of the time, Pallas kernels for 0%

commit v1 on v0

--- a/solution.py
+++ b/solution.py
@@ -2,6 +2,7 @@
 import jax.numpy as jnp
 from jax import lax
 from jax.sharding import PartitionSpec as P
+from jax.lax import psum
 
 
 def extended(block, sides, width):
@@ -65,6 +66,12 @@
 
 
 def on_device(column_features, column_route, cotangent, first_weight, second_weight):
+
+    def match_masks_by_axis(raw):
+        for i0 in ("rx", "ry"):
+            raw = psum(raw, i0)
+        return raw
+
     count_x = lax.axis_size("rx")
     count_y = lax.axis_size("ry")
     count_all = count_x * count_y
@@ -154,7 +161,7 @@
     )
     second_local = correlate(outer_grad, padded_a)
     first_local = correlate(hidden_grad, padded_x)
-    first_total, second_total = lax.psum((first_local, second_local), ("rx", "ry"))
+    first_total, second_total = match_masks_by_axis((first_local, second_local))
     factor = 1.0 / jnp.sqrt(jnp.float32(count_all * shard_rows * depth))
     return (block_output, feature_grads, first_total * factor, second_total * factor)
 

time: 677 us -> 672 us (level)
  waiting for transfers between devices: 131 us -> 122 us
    psum x1 -> x2, waiting for transfers between devices: 121 us -> 112 us  [match_masks_by_axis(): raw = psum(raw, i0)]
  transfers between devices with their start and end apart: 20 -> 21, of which waited for: 5 -> 6; matrix products, arithmetic and copies ran while one was open for 32% -> 33% of each run, Pallas kernels for 0% -> 0%
where the time goes in v1:
time: 672 us; the launch traced here: 664 us
  matrix products  338 us (50%)
  waiting for transfers between devices  122 us (18%)
  local copies, waits for them, and re-layouts  102 us (15%)
  starting transfers between devices  76.5 us (11%)
  between operations  15.3 us (2%)
  other arithmetic  10.5 us (2%)
    dot_general x108, matrix products, conv_sum(): jnp.einsum('xyzi,oi->xyzo', piece, weights[9 * a + 3 * b + c], preferred_...  273 us
    psum x2, waiting for transfers between devices, match_masks_by_axis(): raw = psum(raw, i0)  112 us
    dot_general x54, matrix products, correlate(): jnp.einsum('xyzo,xyzi->oi', grads, piece, preferred_element_type=jnp.floa...  63.1 us
    ppermute x8, starting transfers between devices, extended(): lax.ppermute(lax.slice_in_dim(block, block.shape[dim] - width, None, axis...  28.6 us
    convert_element_type x2, local copies, waits for them, and re-layouts, on_device(): cot_field = jnp.transpose(cotangent.reshape(region_x, region_y, channels,...  15.3 us
  transfers between devices with their start and end apart: 21, of which 6 were waited for; matrix products, arithmetic and copies ran while one was open for 33% of the time, Pallas kernels for 0%

profile of v1, /device:TPU:1, one launch (start us, length us, event | category | flops | bytes accessed | tf_op | source)
XLA Modules:
  0.0 664.2 jit_solution(17765415442161282830)
XLA Ops:
  9.0 11.5 %all-to-all-start = ((s32[128,1,2]{2,1,0:T(1,128)}), s32[128,1,2]{2,1,0:T(1,128)S(1)}, u32[]{:S(2)}, u32[]{:S(2)}) async-start(s32[128,1,2]{2,1,0:T(1,128)} %bitcast), calls=%async_computation | async-start | bytes 131072 | tf_op jit(solution)/shard_map/all_to_all | solution.py:110
  21.0 2.2 copy.39
  24.4 6.9 %reshape.118 = f32[16,16,96,16]{3,2,1,0:T(8,128)} reshape(bf16[16,16,1536]{2,1,0:T(8,128)(2,1)S(1)} %copy-done.16) | data formatting | bytes 2359296 | tf_op jit(solution)/shard_map/convert_element_type | solution.py:130
  31.2 8.4 %copy.37 = f32[16,16,96,16]{2,3,1,0:T(8,128)S(1)} copy(f32[16,16,96,16]{3,2,1,0:T(8,128)} %reshape.118) | data formatting | bytes 3145728 | tf_op jit(solution)/shard_map/convert_element_type | solution.py:130
  39.7 10.2 %all-to-all-start.1 = ((bf16[128,2,1536]{2,1,0:T(2,128)(2,1)}), bf16[128,2,1536]{2,1,0:T(2,128)(2,1)}, u32[]{:S(2)}, u32[]{:S(2)}) async-start(bf16[128,2,1536]{2,1,0:T(2,128)(2,1)} %reshape.103), calls=%async_computation.1 | async-start | bytes 1572864 | tf_op jit(solution)/shard_map/all_to_all | solution.py:103
  52.1 3.5 collective-permute-start.8
  55.6 2.0 reverse_bitcast_fusion
  60.4 1.9 collective-permute-start.9
  62.4 3.8 collective-permute-done.9
  66.4 3.0 collective-permute-start.10
  71.8 3.1 collective-permute-done.11
  76.8 2.6 fusion.61
  93.6 1.9 fusion.70
  95.5 1.8 fusion.71
  115.0 1.8 fusion.75
  120.4 2.3 reshape.104
  123.2 6.7 %reshape.105 = bf16[16,16,96,16]{3,2,1,0:T(8,128)(2,1)} reshape(bf16[256,1536]{1,0:T(8,128)(2,1)S(1)} %convolution_convert_fusion.2) | data formatting | bytes 1572864 | tf_op jit(solution)/shard_map/reshape | solution.py:126
  132.0 4.0 collective-permute-start
  136.1 2.5 fusion.76
  138.6 6.0 copy.34
  144.9 1.9 collective-permute-start.1
  150.5 3.4 collective-permute-start.2
  155.2 2.6 fusion.60
  157.8 6.2 copy.32
  165.6 2.7 reshape.107
  168.4 2.6 fusion.114
  178.1 1.9 fusion.119
  187.1 1.8 fusion.124
  192.5 1.8 fusion.127
  203.2 1.9 fusion.220
  215.7 20.1 %multiply_convert_fusion.1 = (bf16[16,16,16,96]{3,2,1,0:T(8,128)(2,1)}, f32[16,16,16,96]{3,2,1,0:T(8,128)}) fusion(bf16[27,96,96]{2,1,0:T(8,128)(2,1)} %param.8, bf16[18,18,16,96]{3,2,1,0:T(8,128)(2,1)S(1)} %reshape.107, f32[16,16,16,96]{3,2,1,0:T(8,128)} %fusion.208, f32[16,16,16,96]{3,2,1,0:T(8,128)} %fusion.129, f32[16,16,16,96]{3,2,1,0:T(8,128)} %fusion.128, ...), kind=kOutput, calls=%fused_computation.102 | convolution fusion | flops 88080384 | bytes 57906176 | tf_op jit(solution)/shard_map/xyzi,oi->xyzo/dot_general | solution.py:42
  235.8 20.1 %multiply_convert_fusion = bf16[16,16,16,96]{3,2,1,0:T(8,128)(2,1)} fusion(f32[16,16,16,96]{3,2,1,0:T(8,128)} %get-tuple-element.29, f32[16,16,16,96]{3,2,1,0:T(8,128)} %fusion.162, f32[16,16,16,96]{3,2,1,0:T(8,128)} %fusion.76, f32[16,16,16,96]{3,2,1,0:T(8,128)} %fusion.75, f32[16,16,16,96]{3,2,1,0:T(8,128)} %fusion.163, f32[16,16,16,96]{3,2,1,0:T(8,128)} %fusion.74, ...), kind=kOutput, calls=%fused_computation.101 | convolution fusion | flops 89653248 | bytes 58430464 | tf_op jit(solution)/shard_map/xyzi,oi->xyzo/dot_general | solution.py:42
  256.8 2.4 fusion.58
  259.4 2.5 collective-permute-start.4
  262.1 3.2 collective-permute-start.12
  265.3 2.3 fusion.57
  298.4 1.9 collective-permute-start.5
  300.5 1.9 collective-permute-start.13
  304.0 4.0 collective-permute-start.6
  309.6 4.9 collective-permute-start.14
  317.7 2.6 fusion.132
  323.8 1.8 fusion.135
  338.1 1.8 fusion.143
  345.2 1.8 fusion.147
  352.4 1.8 fusion.184
  362.4 2.9 reshape.114
  365.3 2.6 fusion.79
  375.0 1.8 fusion.84
  378.6 1.9 fusion.86
  387.7 1.8 fusion.91
  407.3 1.9 fusion.160
  441.7 20.0 %fusion.1 = bf16[16,16,96,16]{2,3,1,0:T(8,128)(2,1)} fusion(f32[16,16,16,96]{3,2,1,0:T(8,128)} %fusion.153, f32[16,16,16,96]{3,2,1,0:T(8,128)} %fusion.94, f32[16,16,16,96]{3,2,1,0:T(8,128)} %fusion.93, f32[16,16,16,96]{3,2,1,0:T(8,128)} %fusion.154, f32[16,16,16,96]{3,2,1,0:T(8,128)} %fusion.92, f32[16,16,16,96]{3,2,1,0:T(8,128)} %fusion.91, ...), kind=kOutput, calls=%fused_computation.78 | convolution fusion | flops 86900736 | bytes 58430464 | tf_op jit(solution)/shard_map/xyzi,oi->xyzo/dot_general | solution.py:42
  461.6 6.0 copy.40
  467.6 11.3 %reshape.115 = bf16[256,1536]{1,0:T(8,128)(2,1)S(1)} reshape(bf16[16,16,96,16]{3,2,1,0:T(8,128)(2,1)} %copy.40) | data formatting | bytes 1572864 | tf_op jit(solution)/shard_map/reshape | solution.py:147
  481.2 13.2 %all-to-all-start.2 = ((bf16[128,2,1536]{2,1,0:T(2,128)(2,1)}), bf16[128,2,1536]{2,1,0:T(2,128)(2,1)S(1)}, u32[]{:S(2)}, u32[]{:S(2)}) async-start(bf16[128,2,1536]{2,1,0:T(2,128)(2,1)} %reshape.116), calls=%async_computation.2 | async-start | bytes 1572864 | tf_op jit(solution)/shard_map/all_to_all | solution.py:151
  494.4 2.5 fusion.196
  497.0 2.5 fusion.200
  499.5 2.5 fusion.204
  502.0 53.4 %all-reduce.11.cloned.1.call-done = (f32[27,96,96]{2,1,0:T(8,128)}, f32[27,96,96]{2,1,0:T(8,128)}) async-done(((f32[27,96,96]{2,1,0:T(8,128)}, f32[27,96,96]{2,1,0:T(8,128)}), (f32[27,96,96]{2,1,0:T(8,128)}, f32[27,96,96]{2,1,0:T(8,128)})) %all-reduce.11.cloned.1.call-update) | async-done | bytes 1990672 | tf_op jit(solution)/shard_map/psum | solution.py:72
  555.5 19.9 %fusion.4 = bf16[16,16,96,16]{2,3,1,0:T(8,128)(2,1)} fusion(f32[16,16,16,96]{3,2,1,0:T(8,128)} %fusion.172, f32[16,16,16,96]{3,2,1,0:T(8,128)} %fusion.147, f32[16,16,16,96]{3,2,1,0:T(8,128)} %fusion.146, f32[16,16,16,96]{3,2,1,0:T(8,128)} %fusion.176, f32[16,16,16,96]{3,2,1,0:T(8,128)} %fusion.145, f32[16,16,16,96]{3,2,1,0:T(8,128)} %fusion.144, ...), kind=kOutput, calls=%fused_computation.91 | convolution fusion | flops 87293952 | bytes 57119744 | tf_op jit(solution)/shard_map/xyzi,oi->xyzo/dot_general | solution.py:42
  575.4 6.0 copy.36
  581.4 11.8 %reshape.110 = bf16[16,16,1536]{2,1,0:T(8,128)(2,1)} reshape(bf16[16,16,96,16]{3,2,1,0:T(8,128)(2,1)} %copy.36) | data formatting | bytes 1572864 | tf_op jit(solution)/shard_map/reshape | solution.py:141
  594.5 58.9 %all-reduce.9.cloned.1.call-done = (f32[27,96,96]{2,1,0:T(8,128)}, f32[27,96,96]{2,1,0:T(8,128)}) async-done(((f32[27,96,96]{2,1,0:T(8,128)}, f32[27,96,96]{2,1,0:T(8,128)}), (f32[27,96,96]{2,1,0:T(8,128)}, f32[27,96,96]{2,1,0:T(8,128)})) %all-reduce.9.cloned.1.call-update) | async-done | bytes 1990672 | tf_op jit(solution)/shard_map/psum | solution.py:72
  653.4 3.5 broadcast_multiply_fusion
  (264 shorter events, 238.4 us)
Async XLA Ops:
  7.2 13.3 %copy-start = (bf16[128,1536]{1,0:T(8,128)(2,1)S(1)}, bf16[128,1536]{1,0:T(8,128)(2,1)}, u32[]{:S(2)}) copy-start(bf16[128,1536]{1,0:T(8,128)(2,1)} %param.5) | copy-start | bytes 1179652
  8.1 16.3 %copy-start.21 = (s32[128]{0:T(128)}, s32[128]{0:T(128)S(1)}, u32[]{:S(2)}) copy-start(s32[128]{0:T(128)S(1)} %multiply_add_fusion) | copy-start | bytes 1540
  9.0 30.7 %all-to-all-start = ((s32[128,1,2]{2,1,0:T(1,128)}), s32[128,1,2]{2,1,0:T(1,128)S(1)}, u32[]{:S(2)}, u32[]{:S(2)}) async-start(s32[128,1,2]{2,1,0:T(1,128)} %bitcast), calls=%async_computation | async-start | bytes 131072 | tf_op jit(solution)/shard_map/all_to_all | solution.py:110
  20.5 3.8 copy-start.16
  39.7 12.3 %copy-start.2 = (f32[16,16,96,16]{2,3,1,0:T(8,128)}, f32[16,16,96,16]{2,3,1,0:T(8,128)S(1)}, u32[]{:S(2)}) copy-start(f32[16,16,96,16]{2,3,1,0:T(8,128)S(1)} %copy.37) | copy-start | bytes 4718596
  39.7 80.8 %all-to-all-start.1 = ((bf16[128,2,1536]{2,1,0:T(2,128)(2,1)}), bf16[128,2,1536]{2,1,0:T(2,128)(2,1)}, u32[]{:S(2)}, u32[]{:S(2)}) async-start(bf16[128,2,1536]{2,1,0:T(2,128)(2,1)} %reshape.103), calls=%async_computation.1 | async-start | bytes 1572864 | tf_op jit(solution)/shard_map/all_to_all | solution.py:103
  49.9 505.6 %all-reduce.11.cloned.1.call-start = ((), (), s32[]{:S(2)}) async-start(), calls=%async_computation.4 | async-start | bytes 5308416 | tf_op jit(solution)/shard_map/psum | solution.py:72
  51.4 71.3 %copy-start.19 = (s32[256]{0:T(256)}, s32[256]{0:T(256)S(1)}, u32[]{:S(2)}) copy-start(s32[256]{0:T(256)S(1)} %eq.49) | copy-start | bytes 3076
  51.6 6.1 copy-start.17
  51.9 8.3 %copy-start.6 = (bf16[16,16,16,96]{3,2,1,0:T(8,128)(2,1)}, bf16[16,16,16,96]{3,2,1,0:T(8,128)(2,1)S(1)}, u32[]{:S(2)}) copy-start(bf16[16,16,16,96]{3,2,1,0:T(8,128)(2,1)S(1)} %fusion.59) | copy-start | bytes 2359300
  52.1 10.2 %collective-permute-start.8 = (bf16[1,16,1536]{2,1,0:T(8,128)(2,1)S(1)}, bf16[1,16,1536]{2,1,0:T(8,128)(2,1)S(1)}, u32[]{:S(2)}, u32[]{:S(2)}) collective-permute-start(bf16[1,16,1536]{2,1,0:T(8,128)(2,1)S(1)} %slice.931), channel_id=1, source_target_pairs={{0,16},{16,32},{32,48},{48,64},{64,80},{80,96},{96,112},{1,17},{17... | collective-permute-start | bytes 147464 | tf_op jit(solution)/shard_map/ppermute | solution.py:13
  60.4 5.8 collective-permute-start.9
  66.4 5.4 collective-permute-start.10
  69.4 5.5 collective-permute-start.11
  76.8 2.6 copy-start.13
  132.0 16.0 %collective-permute-start = (bf16[1,16,1536]{2,1,0:T(8,128)(2,1)}, bf16[1,16,1536]{2,1,0:T(8,128)(2,1)}, u32[]{:S(2)}, u32[]{:S(2)}) collective-permute-start(bf16[1,16,1536]{2,1,0:T(8,128)(2,1)} %slice.811), channel_id=1, source_target_pairs={{0,16},{16,32},{32,48},{48,64},{64,80},{80,96},{96,112},{1,17},{17... | collective-permute-start | bytes 147464 | tf_op jit(solution)/shard_map/ppermute | solution.py:13
  144.9 5.4 collective-permute-start.1
  150.5 13.4 %collective-permute-start.2 = (bf16[18,1,1536]{2,1,0:T(2,128)(2,1)S(1)}, bf16[18,1,1536]{2,1,0:T(2,128)(2,1)S(1)}, u32[]{:S(2)}, u32[]{:S(2)}) collective-permute-start(bf16[18,1,1536]{2,1,0:T(2,128)(2,1)S(1)} %get-tuple-element.24), channel_id=1, source_target_pairs={{0,1},{1,2},{2,3},{3,4},{4,5},{5,6},{6,7},{7,8},{8,9},{9,10},{10,1... | collective-permute-start | bytes 165896 | tf_op jit(solution)/shard_map/ppermute | solution.py:13
  153.9 10.0 %collective-permute-start.3 = (bf16[18,1,1536]{2,1,0:T(2,128)(2,1)S(1)}, bf16[18,1,1536]{2,1,0:T(2,128)(2,1)S(1)}, u32[]{:S(2)}, u32[]{:S(2)}) collective-permute-start(bf16[18,1,1536]{2,1,0:T(2,128)(2,1)S(1)} %get-tuple-element.25), channel_id=1, source_target_pairs={{1,0},{2,1},{3,2},{4,3},{5,4},{6,5},{7,6},{8,7},{9,8},{10,9},{11,1... | collective-permute-start | bytes 165896 | tf_op jit(solution)/shard_map/ppermute | solution.py:16
  168.4 2.6 copy-start.10
  213.9 1.8 copy-start.18
  256.8 2.5 copy-start.3
  259.4 43.0 %collective-permute-start.4 = (bf16[1,16,1536]{2,1,0:T(8,128)(2,1)S(1)}, bf16[1,16,1536]{2,1,0:T(8,128)(2,1)S(1)}, u32[]{:S(2)}, u32[]{:S(2)}) collective-permute-start(bf16[1,16,1536]{2,1,0:T(8,128)(2,1)S(1)} %slice.871), channel_id=1, source_target_pairs={{0,16},{16,32},{32,48},{48,64},{64,80},{80,96},{96,112},{1,17},{17... | collective-permute-start | bytes 147464 | tf_op jit(solution)/shard_map/ppermute | solution.py:13
  262.1 5.5 copy-start.4
  262.1 47.2 %collective-permute-start.12 = (bf16[1,16,1536]{2,1,0:T(8,128)(2,1)S(1)}, bf16[1,16,1536]{2,1,0:T(8,128)(2,1)S(1)}, u32[]{:S(2)}, u32[]{:S(2)}) collective-permute-start(bf16[1,16,1536]{2,1,0:T(8,128)(2,1)S(1)} %slice.991), channel_id=1, source_target_pairs={{0,16},{16,32},{32,48},{48,64},{64,80},{80,96},{96,112},{1,17},{17... | collective-permute-start | bytes 147464 | tf_op jit(solution)/shard_map/ppermute | solution.py:13
  295.8 1.2 copy-start.5
  298.4 5.4 collective-permute-start.5
  300.5 8.9 %collective-permute-start.13 = (bf16[1,16,1536]{2,1,0:T(8,128)(2,1)S(1)}, bf16[1,16,1536]{2,1,0:T(8,128)(2,1)S(1)}, u32[]{:S(2)}, u32[]{:S(2)}) collective-permute-start(bf16[1,16,1536]{2,1,0:T(8,128)(2,1)S(1)} %slice.993), channel_id=1, source_target_pairs={{16,0},{32,16},{48,32},{64,48},{80,64},{96,80},{112,96},{17,1},{33... | collective-permute-start | bytes 147464 | tf_op jit(solution)/shard_map/ppermute | solution.py:16
  304.0 11.8 %collective-permute-start.6 = (bf16[18,1,1536]{2,1,0:T(2,128)(2,1)S(1)}, bf16[18,1,1536]{2,1,0:T(2,128)(2,1)S(1)}, u32[]{:S(2)}, u32[]{:S(2)}) collective-permute-start(bf16[18,1,1536]{2,1,0:T(2,128)(2,1)S(1)} %get-tuple-element.22), channel_id=1, source_target_pairs={{0,1},{1,2},{2,3},{3,4},{4,5},{5,6},{6,7},{7,8},{8,9},{9,10},{10,1... | collective-permute-start | bytes 165896 | tf_op jit(solution)/shard_map/ppermute | solution.py:13
  308.0 7.8 %collective-permute-start.7 = (bf16[18,1,1536]{2,1,0:T(2,128)(2,1)S(1)}, bf16[18,1,1536]{2,1,0:T(2,128)(2,1)S(1)}, u32[]{:S(2)}, u32[]{:S(2)}) collective-permute-start(bf16[18,1,1536]{2,1,0:T(2,128)(2,1)S(1)} %get-tuple-element.23), channel_id=1, source_target_pairs={{1,0},{2,1},{3,2},{4,3},{5,4},{6,5},{7,6},{8,7},{9,8},{10,9},{11,1... | collective-permute-start | bytes 165896 | tf_op jit(solution)/shard_map/ppermute | solution.py:16
  309.4 6.4 copy-start.14
  309.6 51.1 %collective-permute-start.14 = (bf16[18,1,1536]{2,1,0:T(2,128)(2,1)S(1)}, bf16[18,1,1536]{2,1,0:T(2,128)(2,1)S(1)}, u32[]{:S(2)}, u32[]{:S(2)}) collective-permute-start(bf16[18,1,1536]{2,1,0:T(2,128)(2,1)S(1)} %get-tuple-element.18), channel_id=1, source_target_pairs={{0,1},{1,2},{2,3},{3,4},{4,5},{5,6},{6,7},{7,8},{8,9},{9,10},{10,1... | collective-permute-start | bytes 165896 | tf_op jit(solution)/shard_map/ppermute | solution.py:13
  314.5 46.2 %collective-permute-start.15 = (bf16[18,1,1536]{2,1,0:T(2,128)(2,1)S(1)}, bf16[18,1,1536]{2,1,0:T(2,128)(2,1)S(1)}, u32[]{:S(2)}, u32[]{:S(2)}) collective-permute-start(bf16[18,1,1536]{2,1,0:T(2,128)(2,1)S(1)} %get-tuple-element.19), channel_id=1, source_target_pairs={{1,0},{2,1},{3,2},{4,3},{5,4},{6,5},{7,6},{8,7},{9,8},{10,9},{11,1... | collective-permute-start | bytes 165896 | tf_op jit(solution)/shard_map/ppermute | solution.py:16
  317.6 2.6 copy-start.11
  356.0 1.8 copy-start.7
  358.9 1.8 copy-start.15
  365.3 2.6 copy-start.12
  410.9 1.8 copy-start.8
  478.9 0.7 copy-start.20
  481.2 111.9 %all-to-all-start.2 = ((bf16[128,2,1536]{2,1,0:T(2,128)(2,1)}), bf16[128,2,1536]{2,1,0:T(2,128)(2,1)S(1)}, u32[]{:S(2)}, u32[]{:S(2)}) async-start(bf16[128,2,1536]{2,1,0:T(2,128)(2,1)} %reshape.116), calls=%async_computation.2 | async-start | bytes 1572864 | tf_op jit(solution)/shard_map/all_to_all | solution.py:151
  494.4 159.1 %all-reduce.9.cloned.1.call-start = ((), (), s32[]{:S(2)}) async-start(), calls=%async_computation.3 | async-start | bytes 5308416 | tf_op jit(solution)/shard_map/psum | solution.py:72
  502.0 53.5 %copy-start.9 = (bf16[16,16,96,16]{2,3,1,0:T(8,128)(2,1)S(1)}, bf16[16,16,96,16]{2,3,1,0:T(8,128)(2,1)}, u32[]{:S(2)}) copy-start(bf16[16,16,96,16]{2,3,1,0:T(8,128)(2,1)} %copy.32) | copy-start | bytes 2359300
  581.4 12.1 %copy-start.22 = (s32[128]{0:T(128)S(1)}, s32[128]{0:T(128)}, u32[]{:S(2)}) copy-start(s32[128]{0:T(128)} %copy-done.21) | copy-start | bytes 1540
  653.4 3.5 copy-start.1
Sparse Core Ops, SparseCore 0:
  479.1 76.3 all-reduce.10
  559.0 94.4 all-reduce.8
